TPU v7x, 128 devices: a whole 4x4x4 slice. The times are simulated.
128 devices in a mesh: tm: 8 (over x, core), space: 16 (over z, y).
Axes of the slice: x: 4, y: 4, z: 4, core: 2. Of those that a mesh axis runs over, the one named last changes fastest.
Arguments:
- field: float32 [4096, 128, 256], P('tm', 'space'), may hold values from -6 to 6
- mask: int32 [4096, 128, 256], P('tm', 'space'), may hold values 0 or 1
- noise: float32 [128, 256], P('space'), may hold values from 0.1 to 1
- lat_factor: float32 [128, 128], replicated, may hold values from -1 to 2.5, as said below
- lon_factor: float32 [256, 256], replicated, may hold values from -1 to 2.5, as said below
- time_tiles: float32 [5, 128, 128], replicated, may hold values from -1 to 2.5, as said below
- amplitude: float32 [32], replicated, may hold values from 0.5 to 2
- depth: int32 [32], replicated, may hold values from 0 to 4
Outputs:
- product: float32 [4096, 128, 256], P('tm', 'space')
Inputs may be any that keep to these rules, and one draw needn't show every extreme that they name: `lat_factor`: symmetric. `lon_factor`: symmetric. time_tiles[0] is symmetric.
All inputs are finite; a program needn't handle non-finite values. No bound on the sum of `mask` on one device may be relied on, other than what follows from the above.
Results may differ from a plain program's by a relative error of at most 0.0001.
Values sent between devices are 32-bit elements; how exact they have to be, the bound alone decides.
A program may use at most 192 MiB of HBM per device.

v0:
```python
import functools

import jax
import jax.numpy as jnp
from jax import lax
from jax.experimental import pallas as pl
from jax.experimental.pallas import tpu as pltpu
from jax.sharding import PartitionSpec as P

MESH = pl.DeviceIdType.MESH
F32 = jnp.float32
BF16 = jnp.bfloat16
C = 8
HB = 128
OFFSETS = [(dy, dz) for dz in range(4) for dy in range(4) if (dy, dz) != (0, 0)]


def split(x):
    hi = x.astype(BF16)
    return hi, (x - hi.astype(F32)).astype(BF16)


def dot(a, b):
    return jnp.dot(a, b, preferred_element_type=F32)


def kernel(
    field, mask, noise, lat, lon, tiles, amp, depth, out,
    fbuf, mbuf, a_buf, r_buf, z_buf, y_buf, halo, acc, weights, stage, lon2, lat2,
    field_sem, mask_sem, fwd_send, fwd_recv, back_send, back_recv, halo_send, halo_recv, out_sem,
):
    t = lax.axis_index("tm")
    s = lax.axis_index("space")
    sz, sy = s // 4, s % 4
    peers = [
        lax.rem(sz + dz, 4) * 4 + lax.rem(sy + dy, 4) for dy, dz in OFFSETS
    ]
    right, left = lax.rem(t + 1, 8), lax.rem(t + 7, 8)
    rows = fbuf.shape[1]
    chunk = rows // C
    piece = chunk // 16

    def load(c):
        part = pl.ds(c * chunk, chunk)
        return [
            pltpu.make_async_copy(
                source.at[part, pl.ds(half * 128, 128)], target.at[half, part], sem.at[half, c]
            )
            for source, target, sem in ((field, fbuf, field_sem), (mask, mbuf, mask_sem))
            for half in range(2)
        ]

    for c in range(C):
        for copy in load(c):
            copy.start()

    barrier = pltpu.get_barrier_semaphore()
    for peer in peers:
        pl.semaphore_signal(barrier, inc=1, device_id=(t, peer), device_id_type=MESH)
    for side in (left, right):
        pl.semaphore_signal(barrier, inc=1, device_id=(side, s), device_id_type=MESH)

    hi, lo = split(lon[...])
    lon2[0] = hi
    lon2[1] = lo
    hi, lo = split(lat[...])
    lat2[:, 0:128] = hi
    lat2[:, 128:256] = lo
    pl.semaphore_wait(barrier, len(peers) + 2)

    @pl.loop(0, C)
    def _(c):
        for copy in load(c):
            copy.wait()
        part = pl.ds(pl.multiple_of(c * chunk, chunk), chunk)
        x = jnp.concatenate(
            [mbuf[half, part, :].astype(F32) * fbuf[half, part, :] for half in range(2)], axis=1
        )
        hi, lo = split(x)
        x = dot(hi, lon2[0]) + dot(hi, lon2[1]) + dot(lo, lon2[0])
        for half in range(2):
            a_buf[c, :, half] = x[:, half * 128 : half * 128 + 128].reshape(16, piece, 128)
        for peer in peers:
            pltpu.make_async_remote_copy(
                a_buf.at[c, peer],
                r_buf.at[c, s],
                fwd_send.at[c],
                fwd_recv.at[c],
                device_id=(t, peer),
                device_id_type=MESH,
            ).start()
        pltpu.make_async_copy(a_buf.at[c, s], r_buf.at[c, s], fwd_recv.at[c]).start()

    for side in range(3):
        for j in range(4):
            for i in range(4):
                shift = j - i + (0, -4, 4)[side]
                place = pl.ds(i * HB, HB)
                if abs(shift) > 4:
                    weights[side, j, place, :] = jnp.zeros((HB, 2 * HB), BF16)
                    continue
                to = t * 4 + i
                source = to + shift
                inside = (source >= 0) & (source <= 31)
                source = jnp.clip(source, 0, 31)
                low = jnp.minimum(to, source)
                keep = inside & (abs(shift) <= depth[low])
                factor = jnp.where(keep, amp[to] * amp[source], 0.0)
                tile = tiles[abs(shift)]
                if shift < 0:
                    tile = tile.T
                hi, lo = split(factor * tile)
                weights[side, j, place, 0:HB] = hi
                weights[side, j, place, HB : 2 * HB] = lo

    @pl.loop(0, C)
    def _(c):
        pltpu.make_async_copy(r_buf.at[c], r_buf.at[c], fwd_recv.at[c]).wait()
        for h in range(piece // 8):
            x = jnp.concatenate(
                [r_buf[c, :, half, pl.ds(h * 8, 8), :].reshape(128, 128) for half in range(2)], axis=1
            )
            hi, lo = split(x)
            both = jnp.concatenate([hi, hi], axis=0)
            y = dot(lat2[...], both) + dot(lat2[:, 0:128], lo)
            for half in range(2):
                part = y[:, half * 128 : half * 128 + 128]
                z_buf[c, :, half, pl.ds(h * 8, 8), :] = part.reshape(16, 8, 128)
        land = pl.ds(c * chunk + s * piece, piece)
        for peer in peers:
            pltpu.make_async_remote_copy(
                z_buf.at[c, peer],
                y_buf.at[:, land],
                back_send.at[c],
                back_recv.at[c],
                device_id=(t, peer),
                device_id_type=MESH,
            ).start()
        pltpu.make_async_copy(z_buf.at[c, s], y_buf.at[:, land], back_recv.at[c]).start()

    acc[...] = jnp.zeros_like(acc)

    def halo_copy(c, side):
        part = pl.ds(c * chunk, chunk)
        return pltpu.make_async_remote_copy(
            y_buf.at[:, part],
            halo.at[side, :, part],
            halo_send.at[side, c],
            halo_recv.at[side, c],
            device_id=((right, left)[side], s),
            device_id_type=MESH,
        )

    def arrived(c):
        part = pl.ds(c * chunk, chunk)
        pltpu.make_async_copy(y_buf.at[:, part], y_buf.at[:, part], back_recv.at[c]).wait()
        for side in range(2):
            halo_copy(c, side).start()

    def product(ref, side, j, r):
        x = jnp.concatenate(
            [ref[half, pl.ds(j * (HB * 8) + r, HB, stride=8), :] for half in range(2)], axis=1
        )
        hi, lo = split(x)
        both = jnp.concatenate([hi, hi], axis=0)
        return dot(weights[side, j], both) + dot(weights[side, j, :, 0:HB], lo)

    for j in range(4):
        arrived(2 * j)
        arrived(2 * j + 1)
        if j > 0:
            for c in (2 * j - 2, 2 * j - 1):
                for side in range(2):
                    halo_copy(c, side).wait_recv()

        @pl.loop(0, 8)
        def _(r, j=j):
            total = acc[r] + product(y_buf, 0, j, r)
            if j > 0:
                total += product(halo.at[0], 1, j - 1, r) + product(halo.at[1], 2, j - 1, r)
            acc[r] = total

    for c in (6, 7):
        for side in range(2):
            halo_copy(c, side).wait_recv()

    @pl.loop(0, 8)
    def _(r):
        total = acc[r] + product(halo.at[0], 1, 3, r) + product(halo.at[1], 2, 3, r)
        every = pl.ds(r, rows // 8, stride=8)
        row = lax.broadcasted_iota(jnp.int32, (8, 256), 0)
        noise_row = jnp.sum(jnp.where(row == r, noise[...], 0.0), axis=0, keepdims=True)
        for half in range(2):
            lanes = slice(half * 128, half * 128 + 128)
            stage[half, every, :] = (
                mbuf[half, every, :].astype(F32) * total[:, lanes]
                + noise_row[:, lanes] * fbuf[half, every, :]
            )

    def store(half):
        return pltpu.make_async_copy(
            stage.at[half], out.at[:, pl.ds(half * 128, 128)], out_sem.at[half]
        )

    for half in range(2):
        store(half).start()

    @pl.loop(0, C)
    def _(c):
        sent = a_buf.at[c, pl.ds(0, 15)]
        pltpu.make_async_copy(sent, sent, fwd_send.at[c]).wait()
        pltpu.make_async_copy(sent, sent, back_send.at[c]).wait()
        for side in range(2):
            halo_copy(c, side).wait_send()

    for half in range(2):
        store(half).wait()


def per_device(field, mask, noise, lat_factor, lon_factor, time_tiles, amplitude, depth):
    hours, lats, lons = field.shape
    rows = hours * lats
    piece = rows // C // 16
    anywhere = pl.BlockSpec(memory_space=pl.ANY)
    vmem = pl.BlockSpec(memory_space=pltpu.VMEM)
    smem = pl.BlockSpec(memory_space=pltpu.SMEM)
    dma = pltpu.SemaphoreType.DMA
    result = pl.pallas_call(
        kernel,
        out_shape=jax.ShapeDtypeStruct((rows, lons), F32),
        in_specs=[anywhere, anywhere, vmem, vmem, vmem, vmem, smem, smem],
        out_specs=anywhere,
        scratch_shapes=[
            pltpu.VMEM((2, rows, 128), F32),
            pltpu.VMEM((2, rows, 128), jnp.int32),
            pltpu.VMEM((C, 16, 2, piece, 128), F32),
            pltpu.VMEM((C, 16, 2, piece, 128), F32),
            pltpu.VMEM((C, 16, 2, piece, 128), F32),
            pltpu.VMEM((2, rows, 128), F32),
            pltpu.VMEM((2, 2, rows, 128), F32),
            pltpu.VMEM((lats, hours, lons), F32),
            pltpu.VMEM((3, 4, hours, 2 * HB), BF16),
            pltpu.VMEM((2, rows, 128), F32),
            pltpu.VMEM((2, lons, lons), BF16),
            pltpu.VMEM((128, 256), BF16),
            dma((2, C)), dma((2, C)), dma((C,)), dma((C,)), dma((C,)), dma((C,)),
            dma((2, C)), dma((2, C)), dma((2,)),
        ],
        compiler_params=pltpu.CompilerParams(
            collective_id=0, has_side_effects=True, vmem_limit_bytes=60 << 20
        ),
    )(
        field.reshape(rows, lons), mask.reshape(rows, lons), noise,
        lat_factor, lon_factor, time_tiles, amplitude, depth,
    )
    return result.reshape(hours, lats, lons)


def solution(mesh):
    spread = P("tm", "space", None)
    in_specs = (spread, spread, P("space", None), P(), P(), P(), P(), P())
    return jax.shard_map(
        per_device, mesh=mesh, in_specs=in_specs, out_specs=spread, check_vma=False
    )
```

profile of v0, /device:TPU:1, one launch (start us, length us, event | category | flops | bytes accessed | tf_op | source)
XLA Modules:
  0.0 123.8 jit_solution(17801072803441534028)
XLA Ops:
  0.0 119.3 %shard_map.82 = f32[4096,256]{1,0:T(8,128)} custom-call(f32[4096,256]{1,0:T(8,128)} %bitcast.4, s32[4096,256]{1,0:T(8,128)} %bitcast.5, f32[8,256]{1,0:T(8,128)} %noise.1, f32[128,128]{1,0:T(8,128)} %lat.1, f32[256,256]{1,0:T(8,128)} %lon.1, f32[5,128,128]{2,1,0:T(8,128)} %tiles.1, f32[32]{0:T(128)} %amp.1, s32[32]{0:T(128)} %depth.1), custom_call_target="tpu_custom_call" | custom-call | tf_op jit(solution)/shard_map/pallas_call | solution.py:228
  119.4 4.5 %copy.10 = f32[512,8,256]{2,1,0:T(8,128)} copy(f32[512,8,256]{2,1,0:T(8,128)} %bitcast.3) | data formatting | bytes 8388608
where the time goes:
time: 124 us
  Pallas kernels  119 us (96%)
  local copies, waits for them, and re-layouts  4.47 us (4%)
    pallas_call x1, Pallas kernels, per_device(): pl.pallas_call(kernel, out_shape=jax.ShapeDtypeStruct((rows, lons), F32),...  119 us
    unnamed x1, local copies, waits for them, and re-layouts  4.47 us

commit v1 on v0

v1 whole, which is shorter than its diff:
```python
import jax
import jax.numpy as jnp
from jax import lax
from jax.experimental import pallas as pl
from jax.experimental.pallas import tpu as pltpu
from jax.sharding import PartitionSpec as P

MESH = pl.DeviceIdType.MESH
F32 = jnp.float32
BF16 = jnp.bfloat16
C = 4
HB = 128
OFFSETS = [(dy, dz) for dz in range(4) for dy in range(4) if (dy, dz) != (0, 0)]


def split(x):
    hi = x.astype(BF16)
    return hi, (x - hi.astype(F32)).astype(BF16)


def dot(a, b):
    return jnp.dot(a, b, preferred_element_type=F32)


def kernel(
    field, mask, noise, lat, lon, tiles, amp, depth, out,
    fbuf, mbuf, first, mixed, r_buf, z_buf, wide, y_buf, wh, wl, xh, xl, lon2, lat2,
    field_sem, mask_sem, fwd_send, fwd_recv, back_send, back_recv, halo_send, halo_recv,
):
    t = lax.axis_index("tm")
    s = lax.axis_index("space")
    sz, sy = s // 4, s % 4
    peers = [lax.rem(sz + dz, 4) * 4 + lax.rem(sy + dy, 4) for dy, dz in OFFSETS]
    right, left = lax.rem(t + 1, 8), lax.rem(t + 7, 8)
    rows = fbuf.shape[0]
    chunk = rows // C
    piece = chunk // 16

    def load(c):
        part = pl.ds(c * chunk, chunk)
        return (
            pltpu.make_async_copy(field.at[part], fbuf.at[part], field_sem.at[c]),
            pltpu.make_async_copy(mask.at[part], mbuf.at[part], mask_sem.at[c]),
        )

    for c in range(C):
        for copy in load(c):
            copy.start()

    barrier = pltpu.get_barrier_semaphore()
    for peer in peers:
        pl.semaphore_signal(barrier, inc=1, device_id=(t, peer), device_id_type=MESH)
    for side in (left, right):
        pl.semaphore_signal(barrier, inc=1, device_id=(side, s), device_id_type=MESH)

    hi, lo = split(lon[...])
    lon2[0] = hi
    lon2[1] = lo
    hi, lo = split(lat[...])
    lat2[:, 0:128] = hi
    lat2[:, 128:256] = lo

    def lon_product(c):
        for copy in load(c):
            copy.wait()
        part = pl.ds(pl.multiple_of(c * chunk, chunk), chunk)
        hi, lo = split(mbuf[part, :].astype(F32) * fbuf[part, :])
        x = dot(hi, lon2[0]) + dot(hi, lon2[1]) + dot(lo, lon2[0])
        first[part, :] = x[:, 0:128]
        wide[1, pl.ds(pl.multiple_of(rows + c * chunk, chunk), chunk), :] = x[:, 128:256]

    def send_forward(half, c):
        source = (first, mixed)[half]
        for peer in peers:
            pltpu.make_async_remote_copy(
                source.at[pl.ds((c * 16 + peer) * piece, piece)],
                r_buf.at[half, c, s],
                fwd_send.at[half, c],
                fwd_recv.at[half, c],
                device_id=(t, peer),
                device_id_type=MESH,
            ).start()
        pltpu.make_async_copy(
            source.at[pl.ds((c * 16 + s) * piece, piece)], r_buf.at[half, c, s], fwd_recv.at[half, c]
        ).start()

    def lat_product(half, c):
        got = r_buf.at[half, c]
        pltpu.make_async_copy(got, got, fwd_recv.at[half, c]).wait()
        for h in range(0, piece // 8, 2):
            x = jnp.concatenate(
                [r_buf[half, c, :, pl.ds((h + k) * 8, 8), :].reshape(128, 128) for k in range(2)], axis=1
            )
            hi, lo = split(x)
            y = dot(lat2[...], jnp.concatenate([hi, hi], axis=0)) + dot(lat2[:, 0:128], lo)
            for k in range(2):
                part = y[:, k * 128 : k * 128 + 128]
                z_buf[half, c, :, pl.ds((h + k) * 8, 8), :] = part.reshape(16, 8, 128)
        place = (c * 16 + s) * piece
        target = (wide.at[0, pl.ds(rows + place, piece)], y_buf.at[1, pl.ds(place, piece)])[half]
        for peer in peers:
            pltpu.make_async_remote_copy(
                z_buf.at[half, c, peer],
                target,
                back_send.at[half, c],
                back_recv.at[half, c],
                device_id=(t, peer),
                device_id_type=MESH,
            ).start()
        pltpu.make_async_copy(z_buf.at[half, c, s], target, back_recv.at[half, c]).start()

    def halo_copy(half, c, side):
        return pltpu.make_async_remote_copy(
            wide.at[half, pl.ds(rows + c * chunk, chunk)],
            wide.at[half, pl.ds(2 * side * rows + c * chunk, chunk)],
            halo_send.at[half, side, c],
            halo_recv.at[half, side, c],
            device_id=((right, left)[side], s),
            device_id_type=MESH,
        )

    def time_product(half):
        for c in range(C):
            for side in range(2):
                halo_copy(half, c, side).wait_recv()

        @pl.loop(0, 4)
        def _(p):
            for g in range(12):
                x = jnp.concatenate(
                    [wide[half, pl.ds(g * (HB * 8) + 2 * p + k, HB, stride=8), :] for k in range(2)], axis=1
                )
                hi, lo = split(x)
                xh[pl.ds(g * HB, HB), :] = hi
                xl[pl.ds(g * HB, HB), :] = lo
            x = dot(wh[...], xh[...]) + dot(wl[...], xh[...]) + dot(wh[...], xl[...])
            for k in range(2):
                every = pl.ds(2 * p + k, rows // 8, stride=8)
                part = x[:, k * 128 : k * 128 + 128]
                if half == 0:
                    y_buf[0, every, :] = part
                else:
                    mixed[every, :] = part

    def finish(half, c):
        part = pl.ds(pl.multiple_of(c * chunk, chunk), chunk)
        lanes = slice(half * 128, half * 128 + 128)
        tall = (chunk // 8, 8, 128)
        value = mbuf[part, lanes].astype(F32) * y_buf[half, part, :]
        value = value.reshape(tall) + noise[:, lanes][None] * fbuf[part, lanes].reshape(tall)
        out[part, lanes] = value.reshape(chunk, 128)

    lon_product(0)
    pl.semaphore_wait(barrier, len(peers) + 2)
    send_forward(0, 0)
    for side in range(2):
        halo_copy(1, 0, side).start()

    @pl.loop(1, C)
    def _(c):
        lon_product(c)
        send_forward(0, c)
        for side in range(2):
            halo_copy(1, c, side).start()

    for j in range(12):
        for i in range(4):
            shift = j - 4 - i
            place, across = pl.ds(i * HB, HB), pl.ds(j * HB, HB)
            if abs(shift) > 4:
                wh[place, across] = jnp.zeros((HB, HB), BF16)
                wl[place, across] = jnp.zeros((HB, HB), BF16)
                continue
            to = t * 4 + i
            source = to + shift
            inside = (source >= 0) & (source <= 31)
            source = jnp.clip(source, 0, 31)
            keep = inside & (abs(shift) <= depth[jnp.minimum(to, source)])
            factor = jnp.where(keep, amp[to] * amp[source], 0.0)
            tile = tiles[abs(shift)]
            if shift < 0:
                tile = tile.T
            wh[place, across], wl[place, across] = split(factor * tile)

    @pl.loop(0, C)
    def _(c):
        lat_product(0, c)

    time_product(1)

    @pl.loop(0, C)
    def _(c):
        send_forward(1, c)

    @pl.loop(0, C)
    def _(c):
        got = wide.at[0, pl.ds(rows + c * chunk, chunk)]
        pltpu.make_async_copy(got, got, back_recv.at[0, c]).wait()
        for side in range(2):
            halo_copy(0, c, side).start()

    @pl.loop(0, C)
    def _(c):
        lat_product(1, c)

    time_product(0)

    @pl.loop(0, C)
    def _(c):
        finish(0, c)

    @pl.loop(0, C)
    def _(c):
        got = y_buf.at[1, pl.ds(c * chunk, chunk)]
        pltpu.make_async_copy(got, got, back_recv.at[1, c]).wait()
        finish(1, c)

    @pl.loop(0, C)
    def _(c):
        for half in range(2):
            sent = z_buf.at[half, c, pl.ds(0, 15)]
            pltpu.make_async_copy(sent, sent, fwd_send.at[half, c]).wait()
            pltpu.make_async_copy(sent, sent, back_send.at[half, c]).wait()
            for side in range(2):
                halo_copy(half, c, side).wait_send()


def per_device(field, mask, noise, lat_factor, lon_factor, time_tiles, amplitude, depth):
    hours, lats, lons = field.shape
    rows = hours * lats
    piece = rows // C // 16
    anywhere = pl.BlockSpec(memory_space=pl.ANY)
    vmem = pl.BlockSpec(memory_space=pltpu.VMEM)
    smem = pl.BlockSpec(memory_space=pltpu.SMEM)
    dma = pltpu.SemaphoreType.DMA
    result = pl.pallas_call(
        kernel,
        out_shape=pltpu.VMEM((rows, lons), F32),
        in_specs=[anywhere, anywhere, vmem, vmem, vmem, vmem, smem, smem],
        out_specs=vmem,
        scratch_shapes=[
            pltpu.VMEM((rows, lons), F32),
            pltpu.VMEM((rows, lons), jnp.int32),
            pltpu.VMEM((rows, 128), F32),
            pltpu.VMEM((rows, 128), F32),
            pltpu.VMEM((2, C, 16, piece, 128), F32),
            pltpu.VMEM((2, C, 16, piece, 128), F32),
            pltpu.VMEM((2, 3 * rows, 128), F32),
            pltpu.VMEM((2, rows, 128), F32),
            pltpu.VMEM((hours, 3 * hours), BF16),
            pltpu.VMEM((hours, 3 * hours), BF16),
            pltpu.VMEM((3 * hours, 256), BF16),
            pltpu.VMEM((3 * hours, 256), BF16),
            pltpu.VMEM((2, lons, lons), BF16),
            pltpu.VMEM((128, 256), BF16),
            dma((C,)), dma((C,)),
            dma((2, C)), dma((2, C)), dma((2, C)), dma((2, C)),
            dma((2, 2, C)), dma((2, 2, C)),
        ],
        compiler_params=pltpu.CompilerParams(
            collective_id=0, has_side_effects=True, vmem_limit_bytes=52 << 20
        ),
    )(
        field.reshape(rows, lons), mask.reshape(rows, lons), noise,
        lat_factor, lon_factor, time_tiles, amplitude, depth,
    )
    return result.reshape(hours, lats, lons)


def solution(mesh):
    spread = P("tm", "space", None)
    in_specs = (spread, spread, P("space", None), P(), P(), P(), P(), P())
    return jax.shard_map(
        per_device, mesh=mesh, in_specs=in_specs, out_specs=spread, check_vma=False
    )
```

time: 124 us -> 103 us (0.83)
  Pallas kernels: 119 us -> 101 us
  local copies, waits for them, and re-layouts: 4.47 us -> 2.02 us
    pallas_call x1, Pallas kernels: 119 us -> 101 us  [per_device(): pl.pallas_call(kernel, out_shape=pltpu.VMEM((rows, lons), F32), in_specs=...]
    unnamed x1, local copies, waits for them, and re-layouts: 4.47 us -> 2.02 us
where the time goes in v1:
time: 103 us
  Pallas kernels  101 us (98%)
  local copies, waits for them, and re-layouts  2.02 us (2%)
    pallas_call x1, Pallas kernels, per_device(): pl.pallas_call(kernel, out_shape=pltpu.VMEM((rows, lons), F32), in_specs=...  101 us

profile of v1, /device:TPU:1, one launch (start us, length us, event | category | flops | bytes accessed | tf_op | source)
XLA Modules:
  0.0 102.6 jit_solution(2678453817940712744)
XLA Ops:
  0.0 100.6 %shard_map.82 = f32[4096,256]{1,0:T(8,128)S(1)} custom-call(f32[4096,256]{1,0:T(8,128)} %bitcast.4, s32[4096,256]{1,0:T(8,128)} %bitcast.5, f32[8,256]{1,0:T(8,128)} %noise.1, f32[128,128]{1,0:T(8,128)} %lat.1, f32[256,256]{1,0:T(8,128)} %lon.1, f32[5,128,128]{2,1,0:T(8,128)} %tiles.1, f32[32]{0:T(128)} %amp.1, s32[32]{0:T(128)} %depth.1), custom_call_target="tpu_custom_call" | custom-call | tf_op jit(solution)/shard_map/pallas_call | solution.py:236
  100.6 2.0 %copy.10 = f32[512,8,256]{2,1,0:T(8,128)} copy(f32[512,8,256]{2,1,0:T(8,128)S(1)} %bitcast.3) | data formatting | bytes 8388608

commit v2 on v1

--- a/solution.py
+++ b/solution.py
@@ -10,7 +10,10 @@
 BF16 = jnp.bfloat16
 C = 4
 HB = 128
-OFFSETS = [(dy, dz) for dz in range(4) for dy in range(4) if (dy, dz) != (0, 0)]
+OFFSETS = [
+    (2, 2), (1, 2), (2, 1), (3, 2), (2, 3), (1, 1), (3, 3), (1, 3), (3, 1),
+    (2, 0), (0, 2), (1, 0), (0, 1), (3, 0), (0, 3),
+]
 
 
 def split(x):
@@ -23,9 +26,9 @@
 
 
 def kernel(
-    field, mask, noise, lat, lon, tiles, amp, depth, out,
+    field, mask, noise_in, lat_in, lon_in, tiles_in, amp_in, depth_in, out,
     fbuf, mbuf, first, mixed, r_buf, z_buf, wide, y_buf, wh, wl, xh, xl, lon2, lat2,
-    field_sem, mask_sem, fwd_send, fwd_recv, back_send, back_recv, halo_send, halo_recv,
+    noise, lat, lon, tiles, amp, depth, field_sem, mask_sem, small_sem, fwd_send, fwd_recv, back_send, back_recv, halo_send, halo_recv,
 ):
     t = lax.axis_index("tm")
     s = lax.axis_index("space")
@@ -43,22 +46,29 @@
             pltpu.make_async_copy(mask.at[part], mbuf.at[part], mask_sem.at[c]),
         )
 
-    for c in range(C):
-        for copy in load(c):
-            copy.start()
-
     barrier = pltpu.get_barrier_semaphore()
     for peer in peers:
         pl.semaphore_signal(barrier, inc=1, device_id=(t, peer), device_id_type=MESH)
     for side in (left, right):
         pl.semaphore_signal(barrier, inc=1, device_id=(side, s), device_id_type=MESH)
 
+    small = [
+        pltpu.make_async_copy(source, target, small_sem.at[k])
+        for k, (source, target) in enumerate(
+            ((lon_in, lon), (lat_in, lat), (tiles_in, tiles), (amp_in, amp), (depth_in, depth), (noise_in, noise))
+        )
+    ]
+    small[0].start()
+    for c in range(C):
+        for copy in load(c):
+            copy.start()
+    for copy in small[1:]:
+        copy.start()
+
+    small[0].wait()
     hi, lo = split(lon[...])
     lon2[0] = hi
     lon2[1] = lo
-    hi, lo = split(lat[...])
-    lat2[:, 0:128] = hi
-    lat2[:, 128:256] = lo
 
     def lon_product(c):
         for copy in load(c):
@@ -163,6 +173,12 @@
         for side in range(2):
             halo_copy(1, c, side).start()
 
+    for copy in small[1:]:
+        copy.wait()
+    hi, lo = split(lat[...])
+    lat2[:, 0:128] = hi
+    lat2[:, 128:256] = lo
+
     for j in range(12):
         for i in range(4):
             shift = j - 4 - i
@@ -231,12 +247,11 @@
     piece = rows // C // 16
     anywhere = pl.BlockSpec(memory_space=pl.ANY)
     vmem = pl.BlockSpec(memory_space=pltpu.VMEM)
-    smem = pl.BlockSpec(memory_space=pltpu.SMEM)
     dma = pltpu.SemaphoreType.DMA
     result = pl.pallas_call(
         kernel,
         out_shape=pltpu.VMEM((rows, lons), F32),
-        in_specs=[anywhere, anywhere, vmem, vmem, vmem, vmem, smem, smem],
+        in_specs=[anywhere] * 8,
         out_specs=vmem,
         scratch_shapes=[
             pltpu.VMEM((rows, lons), F32),
@@ -253,7 +268,13 @@
             pltpu.VMEM((3 * hours, 256), BF16),
             pltpu.VMEM((2, lons, lons), BF16),
             pltpu.VMEM((128, 256), BF16),
-            dma((C,)), dma((C,)),
+            pltpu.VMEM(noise.shape, F32),
+            pltpu.VMEM(lat_factor.shape, F32),
+            pltpu.VMEM(lon_factor.shape, F32),
+            pltpu.VMEM(time_tiles.shape, F32),
+            pltpu.SMEM(amplitude.shape, F32),
+            pltpu.SMEM(depth.shape, jnp.int32),
+            dma((C,)), dma((C,)), dma((6,)),
             dma((2, C)), dma((2, C)), dma((2, C)), dma((2, C)),
             dma((2, 2, C)), dma((2, 2, C)),
         ],

time: 103 us -> 101 us (0.981)
  Pallas kernels: 101 us -> 99 us
    pallas_call x1, Pallas kernels: 101 us -> 99 us  [per_device(): pl.pallas_call(kernel, out_shape=pltpu.VMEM((rows, lons), F32), in_specs=...]
where the time goes in v2:
time: 101 us
  Pallas kernels  99 us (98%)
  local copies, waits for them, and re-layouts  2.02 us (2%)
    pallas_call x1, Pallas kernels, per_device(): pl.pallas_call(kernel, out_shape=pltpu.VMEM((rows, lons), F32), in_specs=...  99 us

profile of v2, /device:TPU:1, one launch (start us, length us, event | category | flops | bytes accessed | tf_op | source)
XLA Modules:
  0.0 101.0 jit_solution(3153362145692591230)
XLA Ops:
  0.0 99.0 %shard_map.82 = f32[4096,256]{1,0:T(8,128)S(1)} custom-call(f32[4096,256]{1,0:T(8,128)} %bitcast.4, s32[4096,256]{1,0:T(8,128)} %bitcast.5, f32[8,256]{1,0:T(8,128)} %noise_in.1, f32[128,128]{1,0:T(8,128)} %lat_in.1, f32[256,256]{1,0:T(8,128)} %lon_in.1, f32[5,128,128]{2,1,0:T(8,128)} %tiles_in.1, f32[32]{0:T(128)} %amp_in.1, s32[32]{0:T(128)} %depth_in.1), custom_call_target="tpu_custom_call" | custom-call | tf_op jit(solution)/shard_map/pallas_call | solution.py:251
  99.0 2.0 %copy.10 = f32[512,8,256]{2,1,0:T(8,128)} copy(f32[512,8,256]{2,1,0:T(8,128)S(1)} %bitcast.3) | data formatting | bytes 8388608

commit v3 on v2

--- a/solution.py
+++ b/solution.py
@@ -1,3 +1,5 @@
+import functools
+
 import jax
 import jax.numpy as jnp
 from jax import lax
@@ -108,7 +110,8 @@
                 z_buf[half, c, :, pl.ds((h + k) * 8, 8), :] = part.reshape(16, 8, 128)
         place = (c * 16 + s) * piece
         target = (wide.at[0, pl.ds(rows + place, piece)], y_buf.at[1, pl.ds(place, piece)])[half]
-        for peer in peers:
+
+        def send(peer):
             pltpu.make_async_remote_copy(
                 z_buf.at[half, c, peer],
                 target,
@@ -117,6 +120,16 @@
                 device_id=(t, peer),
                 device_id_type=MESH,
             ).start()
+
+        if half == 0:
+            for peer in peers:
+                send(peer)
+        else:
+            for turn in (True, False):
+                for peer in peers:
+                    early = (peer <= 1) | (peer == 3) | (peer == 4)
+                    pl.when(early if turn else jnp.logical_not(early))(functools.partial(send, peer))
+
         pltpu.make_async_copy(z_buf.at[half, c, s], target, back_recv.at[half, c]).start()
 
     def halo_copy(half, c, side):

time: 101 us -> 101 us (level)
  no operation moved by 1% of the time
where the time goes in v3:
time: 101 us; the launch traced here: 100 us
  Pallas kernels  98.4 us (97%)
  local copies, waits for them, and re-layouts  2.02 us (2%)
    pallas_call x1, Pallas kernels, per_device(): pl.pallas_call(kernel, out_shape=pltpu.VMEM((rows, lons), F32), in_specs=...  98.4 us

profile of v3, /device:TPU:1, one launch (start us, length us, event | category | flops | bytes accessed | tf_op | source)
XLA Modules:
  0.0 100.4 jit_solution(3557137375366593187)
XLA Ops:
  0.0 98.4 %shard_map.82 = f32[4096,256]{1,0:T(8,128)S(1)} custom-call(f32[4096,256]{1,0:T(8,128)} %bitcast.4, s32[4096,256]{1,0:T(8,128)} %bitcast.5, f32[8,256]{1,0:T(8,128)} %noise_in.1, f32[128,128]{1,0:T(8,128)} %lat_in.1, f32[256,256]{1,0:T(8,128)} %lon_in.1, f32[5,128,128]{2,1,0:T(8,128)} %tiles_in.1, f32[32]{0:T(128)} %amp_in.1, s32[32]{0:T(128)} %depth_in.1), custom_call_target="tpu_custom_call" | custom-call | tf_op jit(solution)/shard_map/pallas_call | solution.py:264
  98.4 2.0 %copy.10 = f32[512,8,256]{2,1,0:T(8,128)} copy(f32[512,8,256]{2,1,0:T(8,128)S(1)} %bitcast.3) | data formatting | bytes 8388608

commit v4 on v3

--- a/solution.py
+++ b/solution.py
@@ -238,6 +238,18 @@
     def _(c):
         finish(0, c)
 
+    def sent(sems, half, c):
+        part = z_buf.at[half, c, pl.ds(0, 15)]
+        pltpu.make_async_copy(part, part, sems.at[half, c]).wait()
+
+    @pl.loop(0, C)
+    def _(c):
+        for half in range(2):
+            sent(fwd_send, half, c)
+            for side in range(2):
+                halo_copy(half, c, side).wait_send()
+        sent(back_send, 0, c)
+
     @pl.loop(0, C)
     def _(c):
         got = y_buf.at[1, pl.ds(c * chunk, chunk)]
@@ -246,12 +258,7 @@
 
     @pl.loop(0, C)
     def _(c):
-        for half in range(2):
-            sent = z_buf.at[half, c, pl.ds(0, 15)]
-            pltpu.make_async_copy(sent, sent, fwd_send.at[half, c]).wait()
-            pltpu.make_async_copy(sent, sent, back_send.at[half, c]).wait()
-            for side in range(2):
-                halo_copy(half, c, side).wait_send()
+        sent(back_send, 1, c)
 
 
 def per_device(field, mask, noise, lat_factor, lon_factor, time_tiles, amplitude, depth):

time: 101 us -> 101 us (level)
  no operation moved by 1% of the time
where the time goes in v4:
time: 101 us; the launch traced here: 100 us
  Pallas kernels  98.4 us (97%)
  local copies, waits for them, and re-layouts  2.02 us (2%)
    pallas_call x1, Pallas kernels, per_device(): pl.pallas_call(kernel, out_shape=pltpu.VMEM((rows, lons), F32), in_specs=...  98.4 us

profile of v4, /device:TPU:1, one launch (start us, length us, event | category | flops | bytes accessed | tf_op | source)
XLA Modules:
  0.0 100.4 jit_solution(4358759367179380254)
XLA Ops:
  0.0 98.4 %shard_map.82 = f32[4096,256]{1,0:T(8,128)S(1)} custom-call(f32[4096,256]{1,0:T(8,128)} %bitcast.4, s32[4096,256]{1,0:T(8,128)} %bitcast.5, f32[8,256]{1,0:T(8,128)} %noise_in.1, f32[128,128]{1,0:T(8,128)} %lat_in.1, f32[256,256]{1,0:T(8,128)} %lon_in.1, f32[5,128,128]{2,1,0:T(8,128)} %tiles_in.1, f32[32]{0:T(128)} %amp_in.1, s32[32]{0:T(128)} %depth_in.1), custom_call_target="tpu_custom_call" | custom-call | tf_op jit(solution)/shard_map/pallas_call | solution.py:271
  98.4 2.0 %copy.10 = f32[512,8,256]{2,1,0:T(8,128)} copy(f32[512,8,256]{2,1,0:T(8,128)S(1)} %bitcast.3) | data formatting | bytes 8388608

commit v5 on v3

--- a/solution.py
+++ b/solution.py
@@ -13,8 +13,8 @@
 C = 4
 HB = 128
 OFFSETS = [
-    (2, 2), (1, 2), (2, 1), (3, 2), (2, 3), (1, 1), (3, 3), (1, 3), (3, 1),
-    (2, 0), (0, 2), (1, 0), (0, 1), (3, 0), (0, 3),
+    (2, 2), (1, 2), (3, 2), (0, 2), (2, 1), (1, 1), (3, 1), (0, 1),
+    (2, 3), (1, 3), (3, 3), (0, 3), (2, 0), (1, 0), (3, 0),
 ]
 
 

time: 101 us -> 101 us (level)
  no operation moved by 1% of the time
where the time goes in v5:
time: 101 us; the launch traced here: 100 us
  Pallas kernels  98.3 us (97%)
  local copies, waits for them, and re-layouts  2.02 us (2%)
    pallas_call x1, Pallas kernels, per_device(): pl.pallas_call(kernel, out_shape=pltpu.VMEM((rows, lons), F32), in_specs=...  98.3 us

profile of v5, /device:TPU:1, one launch (start us, length us, event | category | flops | bytes accessed | tf_op | source)
XLA Modules:
  0.0 100.3 jit_solution(5979286190555118257)
XLA Ops:
  0.0 98.3 %shard_map.82 = f32[4096,256]{1,0:T(8,128)S(1)} custom-call(f32[4096,256]{1,0:T(8,128)} %bitcast.4, s32[4096,256]{1,0:T(8,128)} %bitcast.5, f32[8,256]{1,0:T(8,128)} %noise_in.1, f32[128,128]{1,0:T(8,128)} %lat_in.1, f32[256,256]{1,0:T(8,128)} %lon_in.1, f32[5,128,128]{2,1,0:T(8,128)} %tiles_in.1, f32[32]{0:T(128)} %amp_in.1, s32[32]{0:T(128)} %depth_in.1), custom_call_target="tpu_custom_call" | custom-call | tf_op jit(solution)/shard_map/pallas_call | solution.py:264
  98.3 2.0 %copy.10 = f32[512,8,256]{2,1,0:T(8,128)} copy(f32[512,8,256]{2,1,0:T(8,128)S(1)} %bitcast.3) | data formatting | bytes 8388608
